TPU v7x, 256 devices: a whole 4x4x8 slice. The times are simulated.
256 devices in a mesh: blk: 64 (over y_lo, z, x), rep: 4 (over y_hi, core).
Axes of the slice: x: 4, y: 4 (y_hi: 2, y_lo: 2; y = y_hi * 2 + y_lo), z: 8, core: 2. Of those that a mesh axis runs over, the one named last changes fastest.
Arguments:
- features: bfloat16 [262144, 128], P(('blk', 'rep')), may hold values from -6 to 6
- weight: bfloat16 [128, 512], replicated, may hold values from -0.5 to 0.5
- bias: float32 [512], replicated, may hold values from -3 to 3
- tile_values: bfloat16 [262144, 4096], P(('blk', 'rep')), may hold values from -0.125 to 0.125
- tile_cols: int32 [2048, 32], P(('blk', 'rep')), may hold values from 0 to 95, as said below
- tile_counts: int32 [2048], P(('blk', 'rep')), may hold values from 1 to 32, as said below
- out_grad: bfloat16 [262144, 512], P(('blk', 'rep')), may hold values from -6 to 6
Outputs:
- activations: bfloat16 [262144, 512], P(('blk', 'rep'))
- feature_grad: float32 [262144, 128], P(('blk', 'rep'))
- weight_grad: float32 [128, 512], replicated
- bias_grad: float32 [512], replicated
Inputs may be any that keep to these rules, and one draw needn't show every extreme that they name: `tile_cols`: within one row tile the 32 entries are different. `tile_counts`: slots 0 to count - 1 of a row tile are live.
All inputs are finite; a program needn't handle non-finite values.
Results may differ from a plain program's by a relative error of at most 0.0059.
Values may be sent and summed in bfloat16 or wider, within the bound.
No kernel may reach another device: no remote copies, remote signals or barrier semaphores. Data moves between devices by JAX's collectives and lax.ppermute only.
A program may use at most 128 MiB of HBM per device.

v0:
```python
import math
import jax
import jax.numpy as jnp
from jax import lax
from jax.sharding import PartitionSpec as P

TILE = 128
REACH = 1
SLOTS = 32


def passed_along(value, axis, steps):
    count = lax.axis_size(axis)
    pairs = [(source, (source + steps) % count) for source in range(count)]
    return lax.ppermute(value, axis, pairs)


def in_blocks(shard, dim, length):
    before, after = (shard.shape[:dim], shard.shape[dim + 1 :])
    return jnp.moveaxis(shard.reshape(*before, length, -1, *after), dim, 0)


def summed_on_arrival(shard, axis, dim):
    length = lax.axis_size(axis)
    pieces = lax.all_to_all(in_blocks(shard, dim, length), axis, 0, 0, tiled=True)
    return jnp.sum(pieces, axis=0)


def gelu_parts(pre_act):
    inner = 0.7978845608028654 * (pre_act + 0.044715 * pre_act * pre_act * pre_act)
    tangent = jnp.tanh(inner)
    value_part = 0.5 * pre_act * (1.0 + tangent)
    slope = 0.5 * (1.0 + tangent) + 0.5 * pre_act * (
        1.0 - tangent * tangent
    ) * 0.7978845608028654 * (1.0 + 0.134145 * pre_act * pre_act)
    return (value_part, slope)


def on_device(features, weight, bias, tile_values, tile_cols, tile_counts, out_grad):
    rows_dev, in_dim = features.shape
    row_tiles = rows_dev // TILE
    group_size = lax.axis_size("rep")
    block_rows = rows_dev * group_size
    nodes = block_rows * lax.axis_size("blk")
    offsets = list(range(-REACH, REACH + 1))
    pieces = []
    for offset_now in offsets:
        if offset_now == 0:
            pieces.append(features)
        else:
            pieces.append(passed_along(features, "blk", -offset_now))
    stacked = jnp.stack(pieces)
    window = lax.all_gather(stacked, "rep", axis=1, tiled=True).reshape(-1, in_dim)
    window_tiles = window.reshape(-1, TILE, in_dim)
    is_live = jnp.arange(SLOTS)[None, :] < tile_counts[:, None]
    gathered = window_tiles[tile_cols]
    gathered = jnp.where(is_live[:, :, None, None], gathered, jnp.zeros((), gathered.dtype))
    gathered = gathered.reshape(row_tiles, SLOTS * TILE, in_dim)
    values = tile_values.reshape(row_tiles, TILE, SLOTS * TILE)
    summed = jnp.einsum(
        "rik,rkf->rif", values, gathered, preferred_element_type=jnp.float32
    ).reshape(rows_dev, in_dim)
    aggregated = summed.astype(jnp.bfloat16)
    pre_act = jnp.dot(aggregated, weight, preferred_element_type=jnp.float32) + bias
    value_part, slope = gelu_parts(pre_act)
    activations = value_part.astype(jnp.bfloat16)
    pre_grad = (out_grad.astype(jnp.float32) * slope).astype(jnp.bfloat16)
    factor = 1.0 / math.sqrt(nodes)
    local_weight = (
        lax.dot_general(
            aggregated, pre_grad, (((0,), (0,)), ((), ())), preferred_element_type=jnp.float32
        )
        * factor
    )
    local_bias = jnp.sum(pre_grad.astype(jnp.float32), axis=0) * factor
    weight_grad, bias_grad = lax.psum((local_weight, local_bias), ("blk", "rep"))
    row_grad = lax.dot_general(
        pre_grad, weight, (((1,), (1,)), ((), ())), preferred_element_type=jnp.float32
    ).astype(jnp.bfloat16)
    grad_tiles = row_grad.reshape(row_tiles, TILE, in_dim)
    partial_value = jnp.einsum(
        "rik,rif->rkf", values, grad_tiles, preferred_element_type=jnp.float32
    )
    partial_value = partial_value.reshape(row_tiles, SLOTS, TILE, in_dim)
    partial_value = jnp.where(
        is_live[:, :, None, None], partial_value, jnp.zeros((), partial_value.dtype)
    )
    window_count = len(offsets) * block_rows // TILE
    placed = (
        jnp.zeros((window_count, TILE, in_dim), jnp.float32)
        .at[tile_cols.reshape(-1)]
        .add(partial_value.reshape(-1, TILE, in_dim))
    )
    terms = placed.reshape(len(offsets), block_rows, in_dim)
    block_total = terms[REACH]
    for position, offset_now in enumerate(offsets):
        if offset_now != 0:
            block_total = block_total + passed_along(
                terms[position].astype(jnp.bfloat16), "blk", offset_now
            ).astype(jnp.float32)
    feature_grad = summed_on_arrival(block_total, "rep", 0)
    return (activations, feature_grad, weight_grad, bias_grad)


def solution(mesh):
    in_specs = (
        P(("blk", "rep"), None),
        P(),
        P(),
        P(("blk", "rep"), None),
        P(("blk", "rep"), None),
        P(("blk", "rep")),
        P(("blk", "rep"), None),
    )
    out_specs = (P(("blk", "rep"), None), P(("blk", "rep"), None), P(), P())
    return jax.shard_map(
        on_device, mesh=mesh, in_specs=in_specs, out_specs=out_specs, check_vma=False
    )
```

profile of v0, /device:TPU:2, one launch (start us, length us, event | category | flops | bytes accessed | tf_op | source)
XLA Modules:
  0.0 501.1 jit_solution(1405045156096830641)
XLA Ops:
  7.2 0.0 copy-start
  7.2 0.0 all-gather.2.cloned.1.call-start
  7.2 1.6 collective-permute-start
  8.8 0.8 collective-permute-start.1
  9.6 5.9 %collective-permute-done = bf16[1024,128]{1,0:T(8,128)(2,1)S(1)} collective-permute-done((bf16[1024,128]{1,0:T(8,128)(2,1)}, bf16[1024,128]{1,0:T(8,128)(2,1)S(1)}, u32[]{:S(2)}, u32[]{:S(2)}) %collective-permute-start) | collective-permute-done | bytes 262176 | tf_op jit(solution)/shard_map/ppermute | solution.py:15
  15.6 1.2 collective-permute-done.1
  16.8 1.9 pad_maximum_fusion
  18.7 0.0 all-gather.2.cloned.1.call-update
  18.7 0.7 iota_compare_fusion
  19.4 0.1 copy.15
  19.5 0.1 lt.47
  19.6 0.8 reshape.95
  20.4 0.7 compare_select_fusion
  21.1 0.1 reshape.101
  21.2 0.1 broadcast_bitcast_fusion
  21.3 37.8 %all-gather.2.cloned.1.call-done = bf16[3,4096,128]{2,1,0:T(8,128)(2,1)} async-done(((bf16[3,1024,128]{2,1,0:T(8,128)(2,1)}), bf16[3,4096,128]{2,1,0:T(8,128)(2,1)}) %all-gather.2.cloned.1.call-update) | async-done | bytes 3145744 | tf_op jit(solution)/shard_map/all_gather | solution.py:53
  59.0 10.5 %gather_fusion = bf16[256,128,128]{2,1,0:T(8,128)(2,1)} fusion(bf16[96,128,128]{2,1,0:T(8,128)(2,1)} %bitcast.41, s32[1024]{0:T(1024)S(1)} %pad_clamp_fusion), kind=kCustom, calls=%fused_computation | custom fusion | bytes 16778240 | tf_op jit(solution)/shard_map/gather | solution.py:56
  69.6 16.3 %bitcast_select_fusion = bf16[8,4096,128]{2,1,0:T(8,128)(2,1)S(1)} fusion(pred[8,4096]{1,0:T(8,128)(4,1)S(1)} %broadcast_bitcast_fusion, bf16[8,4096,128]{2,1,0:T(8,128)(2,1)} %bitcast.40), kind=kLoop, calls=%fused_computation.3 | loop fusion | flops 4194304 | bytes 16809984 | tf_op jit(solution)/shard_map/jit(_where)/select_n | solution.py:57
  85.9 0.0 copy-start.2
  85.9 0.0 copy-start.3
  85.9 5.8 %convolution_convert_fusion = bf16[8,128,128]{1,2,0:T(8,128)(2,1)S(1)} fusion(bf16[8,128,4096]{2,1,0:T(8,128)(2,1)} %bitcast.36, bf16[8,4096,128]{2,1,0:T(8,128)(2,1)S(1)} %bitcast_select_fusion), kind=kOutput, calls=%fused_computation.18 | convolution fusion | flops 1073872896 | bytes 17039360 | tf_op jit(solution)/shard_map/rik,rkf->rif/dot_general | solution.py:60
  91.7 0.0 slice-start
  91.7 0.0 copy-done
  91.7 0.0 copy-done.2
  91.7 0.0 copy-done.3
  91.7 0.0 slice-start.1
  91.8 2.7 convert_reduce_fusion
  94.5 0.4 convolution_convert_fusion.1
  94.9 0.0 slice-done
  94.9 0.6 slice-done.1
  95.6 8.1 %convolution_bitcast_fusion = f32[8,4096,128]{1,2,0:T(8,128)} fusion(bf16[8,128,128]{2,1,0:T(8,128)(2,1)S(1)} %bitcast.42, bf16[8,128,4096]{2,1,0:T(8,128)(2,1)S(1)} %bitcast.39), kind=kOutput, calls=%fused_computation.2 | convolution fusion | flops 1073741824 | bytes 25427968 | tf_op jit(solution)/shard_map/rik,rif->rkf/dot_general | solution.py:81
  103.7 17.4 %copy.17 = f32[8,4096,128]{2,1,0:T(8,128)} copy(f32[8,4096,128]{1,2,0:T(8,128)} %convolution_bitcast_fusion) | data formatting | bytes 33554432 | tf_op jit(solution)/shard_map/rik,rif->rkf/dot_general | solution.py:81
  121.0 11.6 %broadcast_select_fusion = f32[256,128,128]{2,1,0:T(8,128)} fusion(f32[256,128,128]{2,1,0:T(8,128)} %bitcast.35, pred[256]{0:T(512)(128)(4,1)S(1)} %lt.47), kind=kLoop, calls=%fused_computation.4 | loop fusion | flops 4194304 | bytes 33554688 | tf_op jit(solution)/shard_map/jit(_where)/select_n | solution.py:85
  132.7 3.4 broadcast_in_dim.45
  136.1 52.3 %scatter_fusion = f32[96,128,128]{2,1,0:T(8,128)} fusion(f32[96,128,128]{2,1,0:T(8,128)} %broadcast_in_dim.45, s32[256]{0:T(256)S(1)} %bitcast.50, f32[256,128,128]{2,1,0:T(8,128)} %broadcast_select_fusion), kind=kCustom, calls=%fused_computation.1 | custom fusion | flops 4194304 | bytes 50332672 | tf_op jit(solution)/shard_map/scatter-add | solution.py:92
  188.4 3.5 convert.4
  191.9 0.2 fusion.9
  192.1 0.5 collective-permute-start.2
  192.6 1.6 collective-permute-start.3
  194.2 1.7 slice.19
  195.9 21.5 %collective-permute-done.2 = bf16[4096,128]{1,0:T(8,128)(2,1)S(1)} collective-permute-done((bf16[4096,128]{1,0:T(8,128)(2,1)S(1)}, bf16[4096,128]{1,0:T(8,128)(2,1)S(1)}, u32[]{:S(2)}, u32[]{:S(2)}) %collective-permute-start.2) | collective-permute-done | bytes 1048608 | tf_op jit(solution)/shard_map/ppermute | solution.py:15
  217.4 3.9 collective-permute-done.3
  221.3 1.6 fusion.7
  222.9 3.6 all-to-all-start
  226.5 0.0 copy-start.1
  226.5 0.0 all-reduce.2.cloned.1.call-start
  226.6 1.0 convolution_multiply_fusion
  227.6 0.0 all-reduce.2.cloned.1.call-update
  227.6 96.5 %psum.15 = f32[512]{0:T(512)} all-reduce(f32[512]{0:T(512)S(1)} %broadcast_multiply_fusion), channel_id=1, replica_groups=mesh['blk'=64,'rep'=4] {'blk','rep'}, use_global_device_ids=true, to_apply=%region_4.5 | all-reduce | flops 512 | bytes 4096 | tf_op jit(solution)/shard_map/psum | solution.py:76
  324.1 0.0 all-to-all-done
  324.1 0.9 reduce_sum.18
  325.1 167.6 %all-reduce.2.cloned.1.call-done = f32[128,512]{1,0:T(8,128)} async-done(((f32[128,512]{1,0:T(8,128)}), f32[128,512]{1,0:T(8,128)}) %all-reduce.2.cloned.1.call-update) | async-done | bytes 262160 | tf_op jit(solution)/shard_map/psum | solution.py:76
  492.6 1.7 copy.21
  494.3 0.0 copy-done.1
  (4 shorter events, 0.0 us)
Async XLA Ops:
  7.2 84.6 %copy-start = (bf16[128,512]{1,0:T(8,128)(2,1)S(1)}, bf16[128,512]{1,0:T(8,128)(2,1)}, u32[]{:S(2)}) copy-start(bf16[128,512]{1,0:T(8,128)(2,1)} %param.8) | copy-start | bytes 393220
  7.2 51.9 %all-gather.2.cloned.1.call-start = ((), (), s32[]{:S(2)}) async-start(), calls=%async_computation.1 | async-start | bytes 3932160 | tf_op jit(solution)/shard_map/all_gather | solution.py:53
  7.2 8.3 %collective-permute-start = (bf16[1024,128]{1,0:T(8,128)(2,1)}, bf16[1024,128]{1,0:T(8,128)(2,1)S(1)}, u32[]{:S(2)}, u32[]{:S(2)}) collective-permute-start(bf16[1024,128]{1,0:T(8,128)(2,1)} %param.7), channel_id=1, source_target_pairs={{0,4},{4,8},{8,12},{12,16},{16,20},{20,24},{24,28},{28,32},{32,36}... | collective-permute-start | bytes 786440 | tf_op jit(solution)/shard_map/ppermute | solution.py:15
  8.8 8.0 %collective-permute-start.1 = (bf16[1024,128]{1,0:T(8,128)(2,1)}, bf16[1024,128]{1,0:T(8,128)(2,1)S(1)}, u32[]{:S(2)}, u32[]{:S(2)}) collective-permute-start(bf16[1024,128]{1,0:T(8,128)(2,1)} %param.7), channel_id=1, source_target_pairs={{0,252},{4,0},{8,4},{12,8},{16,12},{20,16},{24,20},{28,24},{32,28}... | collective-permute-start | bytes 786440 | tf_op jit(solution)/shard_map/ppermute | solution.py:15
  85.9 5.9 %copy-start.2 = (bf16[1024,512]{1,0:T(8,128)(2,1)S(1)}, bf16[1024,512]{1,0:T(8,128)(2,1)}, u32[]{:S(2)}) copy-start(bf16[1024,512]{1,0:T(8,128)(2,1)} %param.13) | copy-start | bytes 3145732
  85.9 5.9 %copy-start.3 = (f32[512]{0:T(512)S(1)}, f32[512]{0:T(512)}, u32[]{:S(2)}) copy-start(f32[512]{0:T(512)} %param.9) | copy-start | bytes 6148
  91.7 3.2 slice-start
  91.7 3.8 slice-start.1
  192.1 25.3 %collective-permute-start.2 = (bf16[4096,128]{1,0:T(8,128)(2,1)S(1)}, bf16[4096,128]{1,0:T(8,128)(2,1)S(1)}, u32[]{:S(2)}, u32[]{:S(2)}) collective-permute-start(bf16[4096,128]{1,0:T(8,128)(2,1)S(1)} %bitcast.46), channel_id=1, source_target_pairs={{0,252},{4,0},{8,4},{12,8},{16,12},{20,16},{24,20},{28,24},{32,28}... | collective-permute-start | bytes 3145736 | tf_op jit(solution)/shard_map/ppermute | solution.py:15
  192.6 28.7 %collective-permute-start.3 = (bf16[4096,128]{1,0:T(8,128)(2,1)S(1)}, bf16[4096,128]{1,0:T(8,128)(2,1)S(1)}, u32[]{:S(2)}, u32[]{:S(2)}) collective-permute-start(bf16[4096,128]{1,0:T(8,128)(2,1)S(1)} %bitcast.45), channel_id=1, source_target_pairs={{0,4},{4,8},{8,12},{12,16},{16,20},{20,24},{24,28},{28,32},{32,36}... | collective-permute-start | bytes 3145736 | tf_op jit(solution)/shard_map/ppermute | solution.py:15
  222.9 101.3 %all-to-all-start = ((f32[4,1024,128]{2,1,0:T(8,128)}), f32[4,1024,128]{2,1,0:T(8,128)S(1)}, u32[]{:S(2)}, u32[]{:S(2)}) async-start(f32[4,1024,128]{2,1,0:T(8,128)} %bitcast.16), calls=%async_computation | async-start | bytes 4194304 | tf_op jit(solution)/shard_map/all_to_all | solution.py:25
  226.5 267.8 %copy-start.1 = (bf16[128,512]{1,0:T(8,128)(2,1)S(1)}, bf16[128,512]{1,0:T(8,128)(2,1)}, u32[]{:S(2)}) copy-start(bf16[128,512]{1,0:T(8,128)(2,1)} %param.8) | copy-start | bytes 393220
  226.5 266.1 %all-reduce.2.cloned.1.call-start = ((), (), s32[]{:S(2)}) async-start(), calls=%async_computation.2 | async-start | bytes 524288 | tf_op jit(solution)/shard_map/psum | solution.py:76
Sparse Core Ops, SparseCore 0:
  18.8 40.1 all-gather.1
  233.3 259.2 all-reduce.1
where the time goes:
time: 502 us; the launch traced here: 501 us
  waiting for transfers between devices  238 us (47%)
  blocking collectives  96.5 us (19%)
  other arithmetic  89.6 us (18%)
  local copies, waits for them, and re-layouts  36.7 us (7%)
  matrix products  18.1 us (4%)
  between operations  14.2 us (3%)
  starting transfers between devices  8.2 us (2%)
    psum x1, waiting for transfers between devices, on_device(): lax.psum((local_weight, local_bias), ('blk', 'rep'))  168 us
    psum x1, blocking collectives, on_device(): lax.psum((local_weight, local_bias), ('blk', 'rep'))  96.5 us
    scatter-add x1, other arithmetic, on_device(): placed = jnp.zeros((window_count, TILE, in_dim), jnp.float32).at[tile_col...  52.3 us
    all_gather x1, waiting for transfers between devices, on_device(): lax.all_gather(stacked, 'rep', axis=1, tiled=True).reshape(-1, in_dim)  37.8 us
    ppermute x4, waiting for transfers between devices, passed_along(): return lax.ppermute(value, axis, pairs)  32.5 us
    dot_general x1, local copies, waits for them, and re-layouts, on_device(): jnp.einsum('rik,rif->rkf', values, grad_tiles, preferred_element_type=jnp...  17.4 us
    select_n x1, other arithmetic, on_device(): jnp.where(is_live[:, :, None, None], gathered, jnp.zeros((), gathered.dty...  16.3 us
    select_n x1, other arithmetic, on_device(): jnp.where(is_live[:, :, None, None], partial_value, jnp.zeros((), partial...  11.6 us
  transfers between devices with their start and end apart: 7, of which 6 were waited for; matrix products, arithmetic and copies ran while one was open for 1% of the time, Pallas kernels for 0%

commit v1 on v0

--- a/solution.py
+++ b/solution.py
@@ -73,7 +73,9 @@
         * factor
     )
     local_bias = jnp.sum(pre_grad.astype(jnp.float32), axis=0) * factor
-    weight_grad, bias_grad = lax.psum((local_weight, local_bias), ("blk", "rep"))
+    weight_grad, bias_grad = lax.psum(
+        lax.psum((local_weight, local_bias), axis_name="rep"), axis_name="blk"
+    )
     row_grad = lax.dot_general(
         pre_grad, weight, (((1,), (1,)), ((), ())), preferred_element_type=jnp.float32
     ).astype(jnp.bfloat16)

time: 502 us -> 848 us (1.69)
  waiting for transfers between devices: 238 us -> 517 us
  blocking collectives: 96.5 us -> 162 us
    psum x1 -> x2, waiting for transfers between devices: 168 us -> 447 us  [the longest x1 397 us: on_device(): lax.psum(lax.psum((local_weight, local_bias), axis_name='rep'), axis_name...]
    psum x1 -> x2, blocking collectives: 96.5 us -> 162 us  [the longest x1 154 us: on_device(): lax.psum(lax.psum((local_weight, local_bias), axis_name='rep'), axis_name...]
  transfers between devices with their start and end apart: 7 -> 8, of which waited for: 6 -> 7; matrix products, arithmetic and copies ran while one was open for 1% -> 1% of each run, Pallas kernels for 0% -> 0%
where the time goes in v1:
time: 848 us; the launch traced here: 846 us
  waiting for transfers between devices  517 us (61%)
  blocking collectives  162 us (19%)
  other arithmetic  89.7 us (11%)
  local copies, waits for them, and re-layouts  36.7 us (4%)
  matrix products  18.1 us (2%)
  between operations  13.9 us (2%)
    psum x1, waiting for transfers between devices, on_device(): lax.psum(lax.psum((local_weight, local_bias), axis_name='rep'), axis_name...  397 us
    psum x1, blocking collectives, on_device(): lax.psum(lax.psum((local_weight, local_bias), axis_name='rep'), axis_name...  154 us
    scatter-add x1, other arithmetic, on_device(): placed = jnp.zeros((window_count, TILE, in_dim), jnp.float32).at[tile_col...  52.5 us
    psum x1, waiting for transfers between devices, on_device(): lax.psum((local_weight, local_bias), axis_name='rep')  50.5 us
    all_gather x1, waiting for transfers between devices, on_device(): lax.all_gather(stacked, 'rep', axis=1, tiled=True).reshape(-1, in_dim)  37.8 us
    ppermute x4, waiting for transfers between devices, passed_along(): return lax.ppermute(value, axis, pairs)  32.6 us
    dot_general x1, local copies, waits for them, and re-layouts, on_device(): jnp.einsum('rik,rif->rkf', values, grad_tiles, preferred_element_type=jnp...  17.4 us
  transfers between devices with their start and end apart: 8, of which 7 were waited for; matrix products, arithmetic and copies ran while one was open for 1% of the time, Pallas kernels for 0%

profile of v1, /device:TPU:2, one launch (start us, length us, event | category | flops | bytes accessed | tf_op | source)
XLA Modules:
  0.0 846.2 jit_solution(17055073306088103983)
XLA Ops:
  7.2 0.0 copy-start
  7.2 0.0 all-gather.2.cloned.1.call-start
  7.2 1.6 collective-permute-start
  8.8 0.8 collective-permute-start.1
  9.6 5.9 collective-permute-done
  15.6 1.2 collective-permute-done.1
  16.8 1.9 pad_maximum_fusion
  18.7 0.0 all-gather.2.cloned.1.call-update
  18.7 0.7 iota_compare_fusion
  19.4 0.1 copy.15
  19.5 0.1 lt.47
  19.6 0.8 reshape.95
  20.4 0.7 compare_select_fusion
  21.1 0.1 reshape.101
  21.2 0.1 broadcast_bitcast_fusion
  21.3 37.8 %all-gather.2.cloned.1.call-done = bf16[3,4096,128]{2,1,0:T(8,128)(2,1)} async-done(((bf16[3,1024,128]{2,1,0:T(8,128)(2,1)}), bf16[3,4096,128]{2,1,0:T(8,128)(2,1)}) %all-gather.2.cloned.1.call-update) | async-done | bytes 3145744 | tf_op jit(solution)/shard_map/all_gather | solution.py:53
  59.0 10.5 %gather_fusion = bf16[256,128,128]{2,1,0:T(8,128)(2,1)} fusion(bf16[96,128,128]{2,1,0:T(8,128)(2,1)} %bitcast.41, s32[1024]{0:T(1024)S(1)} %pad_clamp_fusion), kind=kCustom, calls=%fused_computation | custom fusion | bytes 16778240 | tf_op jit(solution)/shard_map/gather | solution.py:56
  69.5 16.3 %bitcast_select_fusion = bf16[8,4096,128]{2,1,0:T(8,128)(2,1)S(1)} fusion(pred[8,4096]{1,0:T(8,128)(4,1)S(1)} %broadcast_bitcast_fusion, bf16[8,4096,128]{2,1,0:T(8,128)(2,1)} %bitcast.40), kind=kLoop, calls=%fused_computation.3 | loop fusion | flops 4194304 | bytes 16809984 | tf_op jit(solution)/shard_map/jit(_where)/select_n | solution.py:57
  85.8 0.0 copy-start.2
  85.9 0.0 copy-start.3
  85.9 5.8 convolution_convert_fusion
  91.7 0.0 slice-start
  91.7 0.0 copy-done
  91.7 0.0 copy-done.2
  91.7 0.0 copy-done.3
  91.7 0.0 slice-start.1
  91.7 2.7 convert_reduce_fusion
  94.5 0.4 convolution_convert_fusion.1
  94.9 0.0 slice-done
  94.9 0.6 slice-done.1
  95.5 8.1 convolution_bitcast_fusion
  103.6 17.4 %copy.17 = f32[8,4096,128]{2,1,0:T(8,128)} copy(f32[8,4096,128]{1,2,0:T(8,128)} %convolution_bitcast_fusion) | data formatting | bytes 33554432 | tf_op jit(solution)/shard_map/rik,rif->rkf/dot_general | solution.py:83
  121.0 11.6 %broadcast_select_fusion = f32[256,128,128]{2,1,0:T(8,128)} fusion(f32[256,128,128]{2,1,0:T(8,128)} %bitcast.35, pred[256]{0:T(512)(128)(4,1)S(1)} %lt.47), kind=kLoop, calls=%fused_computation.4 | loop fusion | flops 4194304 | bytes 33554688 | tf_op jit(solution)/shard_map/jit(_where)/select_n | solution.py:87
  132.6 3.4 broadcast_in_dim.45
  136.1 52.5 %scatter_fusion = f32[96,128,128]{2,1,0:T(8,128)} fusion(f32[96,128,128]{2,1,0:T(8,128)} %broadcast_in_dim.45, s32[256]{0:T(256)S(1)} %bitcast.50, f32[256,128,128]{2,1,0:T(8,128)} %broadcast_select_fusion), kind=kCustom, calls=%fused_computation.1 | custom fusion | flops 4194304 | bytes 50332672 | tf_op jit(solution)/shard_map/scatter-add | solution.py:94
  188.5 3.5 convert.4
  192.0 0.2 fusion.9
  192.2 0.5 collective-permute-start.2
  192.7 1.6 collective-permute-start.3
  194.3 1.7 slice.19
  196.0 21.4 %collective-permute-done.2 = bf16[4096,128]{1,0:T(8,128)(2,1)S(1)} collective-permute-done((bf16[4096,128]{1,0:T(8,128)(2,1)S(1)}, bf16[4096,128]{1,0:T(8,128)(2,1)S(1)}, u32[]{:S(2)}, u32[]{:S(2)}) %collective-permute-start.2) | collective-permute-done | bytes 1048608 | tf_op jit(solution)/shard_map/ppermute | solution.py:15
  217.5 4.0 collective-permute-done.3
  221.5 1.6 fusion.7
  223.1 3.6 all-to-all-start
  226.7 0.0 copy-start.1
  226.7 0.0 all-reduce.3.cloned.1.call-start
  226.8 1.0 convolution_multiply_fusion
  227.8 0.0 all-reduce.3.cloned.1.call-update
  227.8 0.0 all-reduce.5.cloned.1.call-start
  227.9 50.5 %all-reduce.3.cloned.1.call-done = f32[128,512]{1,0:T(8,128)} async-done(((f32[128,512]{1,0:T(8,128)}), f32[128,512]{1,0:T(8,128)}) %all-reduce.3.cloned.1.call-update) | async-done | bytes 262160 | tf_op jit(solution)/shard_map/psum | solution.py:77
  278.4 0.0 all-reduce.5.cloned.1.call-update
  278.4 7.7 psum.30
  286.1 154.4 %psum.31 = f32[512]{0:T(512)} all-reduce(f32[512]{0:T(512)S(1)} %psum.30), channel_id=1, replica_groups=mesh['blk'=64,'rep'=4] {'blk'}, use_global_device_ids=true, to_apply=%region_6.7 | all-reduce | flops 512 | bytes 4096 | tf_op jit(solution)/shard_map/psum | solution.py:76
  440.5 0.0 all-to-all-done
  440.5 0.9 reduce_sum.18
  441.5 396.5 %all-reduce.5.cloned.1.call-done = f32[128,512]{1,0:T(8,128)} async-done(((f32[128,512]{1,0:T(8,128)}), f32[128,512]{1,0:T(8,128)}) %all-reduce.5.cloned.1.call-update) | async-done | bytes 262160 | tf_op jit(solution)/shard_map/psum | solution.py:76
  838.0 1.7 copy.22
  839.7 0.0 copy-done.1
  (4 shorter events, 0.0 us)
Async XLA Ops:
  7.2 84.5 %copy-start = (bf16[128,512]{1,0:T(8,128)(2,1)S(1)}, bf16[128,512]{1,0:T(8,128)(2,1)}, u32[]{:S(2)}) copy-start(bf16[128,512]{1,0:T(8,128)(2,1)} %param.8) | copy-start | bytes 393220
  7.2 51.9 %all-gather.2.cloned.1.call-start = ((), (), s32[]{:S(2)}) async-start(), calls=%async_computation.1 | async-start | bytes 3932160 | tf_op jit(solution)/shard_map/all_gather | solution.py:53
  7.2 8.3 collective-permute-start
  8.8 8.0 collective-permute-start.1
  85.8 5.9 copy-start.2
  85.9 5.9 copy-start.3
  91.7 3.2 slice-start
  91.7 3.8 slice-start.1
  192.2 25.3 %collective-permute-start.2 = (bf16[4096,128]{1,0:T(8,128)(2,1)S(1)}, bf16[4096,128]{1,0:T(8,128)(2,1)S(1)}, u32[]{:S(2)}, u32[]{:S(2)}) collective-permute-start(bf16[4096,128]{1,0:T(8,128)(2,1)S(1)} %bitcast.46), channel_id=1, source_target_pairs={{0,252},{4,0},{8,4},{12,8},{16,12},{20,16},{24,20},{28,24},{32,28}... | collective-permute-start | bytes 3145736 | tf_op jit(solution)/shard_map/ppermute | solution.py:15
  192.7 28.7 %collective-permute-start.3 = (bf16[4096,128]{1,0:T(8,128)(2,1)S(1)}, bf16[4096,128]{1,0:T(8,128)(2,1)S(1)}, u32[]{:S(2)}, u32[]{:S(2)}) collective-permute-start(bf16[4096,128]{1,0:T(8,128)(2,1)S(1)} %bitcast.45), channel_id=1, source_target_pairs={{0,4},{4,8},{8,12},{12,16},{16,20},{20,24},{24,28},{28,32},{32,36}... | collective-permute-start | bytes 3145736 | tf_op jit(solution)/shard_map/ppermute | solution.py:15
  223.1 217.4 %all-to-all-start = ((f32[4,1024,128]{2,1,0:T(8,128)}), f32[4,1024,128]{2,1,0:T(8,128)S(1)}, u32[]{:S(2)}, u32[]{:S(2)}) async-start(f32[4,1024,128]{2,1,0:T(8,128)} %bitcast.16), calls=%async_computation | async-start | bytes 4194304 | tf_op jit(solution)/shard_map/all_to_all | solution.py:25
  226.7 613.0 %copy-start.1 = (bf16[128,512]{1,0:T(8,128)(2,1)S(1)}, bf16[128,512]{1,0:T(8,128)(2,1)}, u32[]{:S(2)}) copy-start(bf16[128,512]{1,0:T(8,128)(2,1)} %param.8) | copy-start | bytes 393220
  226.7 51.7 %all-reduce.3.cloned.1.call-start = ((), (), s32[]{:S(2)}) async-start(), calls=%async_computation.2 | async-start | bytes 524288 | tf_op jit(solution)/shard_map/psum | solution.py:77
  227.8 610.2 %all-reduce.5.cloned.1.call-start = ((), (), s32[]{:S(2)}) async-start(), calls=%async_computation.3 | async-start | bytes 524288 | tf_op jit(solution)/shard_map/psum | solution.py:76
Sparse Core Ops, SparseCore 0:
  18.8 40.1 all-gather.1
  230.7 47.6 all-reduce.2
  281.0 556.9 all-reduce.4
